TPU v7x, 256 devices: a whole 4x4x8 slice. The times are simulated.
256 devices in a mesh: code: 32 (over y, z), dp: 8 (over x, core).
Axes of the slice: x: 4, y: 4, z: 8, core: 2. Of those that a mesh axis runs over, the one named last changes fastest.
Arguments:
- codebook: bfloat16 [262144, 768], P(('code', 'dp')), may hold values from -6 to 6
- weight_in: bfloat16 [768, 1024], replicated, may hold values from -0.21875 to 0.21875
- bias_in: float32 [1024], replicated, may hold values from -3 to 3
- weight_out: bfloat16 [1024, 256], replicated, may hold values from -0.1875 to 0.1875
- bias_out: float32 [256], replicated, may hold values from -3 to 3
- latents: float32 [262144, 256], P(('code', 'dp')), may hold values from -6 to 6
- cotangent: float32 [262144, 256], P(('code', 'dp')), may hold values from -6 to 6
- code_owner: int32 [262144, 1], P(('code', 'dp')), may hold values from 0 to 255; in each aligned block of 1024 rows (0 to 1023, 1024 to 2047, ...) at most 8 rows name the same one
- code_row: int32 [262144], P(('code', 'dp')), may hold values from 0 to 1023
Outputs:
- latent_grad: float32 [262144, 256], P(('code', 'dp'))
- grad_weight_in: float32 [768, 1024], replicated
- grad_bias_in: float32 [1024], replicated
- grad_weight_out: float32 [1024, 256], replicated
- grad_bias_out: float32 [256], replicated
Inputs may be any that keep to these rules, and one draw needn't show every extreme that they name: In the rows of one device no owner is named by more than 8 rows, a bound that some block reaches; a latent's code is code_owner * 1024 + code_row.
All inputs are finite; a program needn't handle non-finite values.
Results may differ from a plain program's by a relative error of at most 0.0023.
Values sent between devices are 32-bit elements; how exact they have to be, the bound alone decides.
A program may use at most 128 MiB of HBM per device.

v0:
```python
import jax
import jax.numpy as jnp
from jax import lax
from jax.sharding import PartitionSpec as P

scale_gelu = 0.7978845608028654
cubic_term = 0.044715


def in_blocks(array, dim, size):
    before, after = (array.shape[:dim], array.shape[dim + 1 :])
    return jnp.moveaxis(array.reshape(*before, size, -1, *after), dim, 0)


def in_order(tiles, dim):
    shape = list(tiles.shape[1:])
    shape[dim] *= tiles.shape[0]
    return jnp.moveaxis(tiles, 0, dim).reshape(shape)


def exchange_both(array, axis, axes, splits, concats):
    sizes = [lax.axis_size(a) for a in axes]
    tiles = in_blocks(array, splits[0], sizes[0])
    tiles = jnp.moveaxis(in_blocks(tiles, splits[1] + 1, sizes[1]), 0, 1)
    inside = tiles.shape[2:]
    tiles = tiles.reshape(-1, *inside)
    tiles = lax.all_to_all(tiles, axis, split_axis=0, concat_axis=0, tiled=True)
    tiles = in_order(tiles.reshape(*sizes, *inside), concats[0] + 1)
    return in_order(tiles, concats[1])


def gelu_value(x):
    inner = scale_gelu * (x + cubic_term * x * x * x)
    return 0.5 * x * (1.0 + jnp.tanh(inner))


def gelu_slope(x):
    tangent = jnp.tanh(scale_gelu * (x + cubic_term * x * x * x))
    return 0.5 * (1.0 + tangent) + 0.5 * x * (1.0 - tangent * tangent) * scale_gelu * (
        1.0 + 3.0 * cubic_term * x * x
    )


def per_device(
    codebook, weight_in, bias_in, weight_out, bias_out, latents, cotangent, code_owner, code_row
):
    preact = jnp.dot(codebook, weight_in, preferred_element_type=jnp.float32) + bias_in
    hidden = gelu_value(preact).astype(jnp.bfloat16)
    projected = jnp.dot(hidden, weight_out, preferred_element_type=jnp.float32) + bias_out
    n_code = lax.axis_size("code")
    n_data = lax.axis_size("dp")
    devices = n_code * n_data
    owners = code_owner[:, 0]
    count = owners.shape[0]
    width = latents.shape[1]
    capacity = max(2, 2 * count // devices)
    position = jnp.arange(count, dtype=jnp.int32)
    same = (owners[:, None] == owners[None, :]) & (position[None, :] < position[:, None])
    ranks = jnp.sum(same.astype(jnp.int32), axis=1)
    slots = owners * capacity + ranks
    wanted = jnp.full((devices * capacity,), -1, jnp.int32).at[slots].set(code_row)
    wanted = exchange_both(
        wanted.reshape(n_code, n_data, capacity), ("code", "dp"), ("code", "dp"), (0, 1), (0, 1)
    )
    valid = wanted >= 0
    row_ids = jnp.maximum(wanted, 0).reshape(-1)
    picked = jnp.take(projected, row_ids, axis=0).reshape(n_code, n_data, capacity, width)
    picked = jnp.where(valid[..., None], picked, 0.0)
    answers = exchange_both(picked, ("code", "dp"), ("code", "dp"), (0, 1), (0, 1))
    chosen = jnp.take(answers.reshape(devices * capacity, width), slots, axis=0)
    residual = chosen - latents
    latent_grad = cotangent - 0.25 * residual
    outgoing = (
        jnp.zeros((devices * capacity, width), jnp.float32).at[slots].set(cotangent + residual)
    )
    incoming = exchange_both(
        outgoing.reshape(n_code, n_data, capacity, width),
        ("code", "dp"),
        ("code", "dp"),
        (0, 1),
        (0, 1),
    )
    code_grad = jax.ops.segment_sum(
        incoming.reshape(devices * capacity, width), row_ids, num_segments=projected.shape[0]
    )
    code_low = code_grad.astype(jnp.bfloat16)
    gw_out = lax.dot_general(
        hidden, code_low, (((0,), (0,)), ((), ())), preferred_element_type=jnp.float32
    )
    back = lax.dot_general(
        code_low, weight_out, (((1,), (1,)), ((), ())), preferred_element_type=jnp.float32
    )
    preact_grad = (back * gelu_slope(preact)).astype(jnp.bfloat16)
    gb_in = jnp.sum(preact_grad.astype(jnp.float32), axis=0)
    gw_in = lax.dot_general(
        codebook, preact_grad, (((0,), (0,)), ((), ())), preferred_element_type=jnp.float32
    )
    gb_out = jnp.sum(code_grad, axis=0)
    gw_in, gb_in, gw_out, gb_out = lax.psum((gw_in, gb_in, gw_out, gb_out), ("code", "dp"))
    return (latent_grad, gw_in, gb_in, gw_out, gb_out)


def solution(mesh):
    placed = (
        P(("code", "dp"), None),
        P(),
        P(),
        P(),
        P(),
        P(("code", "dp"), None),
        P(("code", "dp"), None),
        P(("code", "dp"), None),
        P(("code", "dp")),
    )
    return jax.shard_map(
        per_device,
        mesh=mesh,
        in_specs=placed,
        out_specs=(P(("code", "dp"), None), P(), P(), P(), P()),
        check_vma=False,
    )
```

profile of v0, /device:TPU:97, one launch (start us, length us, event | category | flops | bytes accessed | tf_op | source)
XLA Modules:
  0.0 492.3 jit_solution(8340644630260382695)
XLA Ops:
  7.2 0.0 copy-start
  7.2 1.3 convert_reduce_fusion.1
  8.5 0.7 and_reduce_fusion
  9.2 4.5 scatter_custom_fusion
  13.7 0.8 reshape_transpose_transpose_reshape_reshape_reshape.6
  14.5 14.3 %all-to-all-start = ((s32[256,1,1,8]{3,2,1,0:T(1,128)}), s32[256,1,1,8]{3,2,1,0:T(1,128)S(1)}, u32[]{:S(2)}, u32[]{:S(2)}) async-start(s32[256,1,1,8]{3,2,1,0:T(1,128)} %bitcast.3), calls=%async_computation | async-start | bytes 262144 | tf_op jit(solution)/shard_map/all_to_all | solution.py:27
  28.8 0.0 copy-done
  28.8 0.0 copy-start.3
  28.8 0.0 copy-start.5
  28.8 5.9 %multiply_convert_fusion = (bf16[1024,1024]{1,0:T(8,128)(2,1)S(1)}, f32[1024,1024]{1,0:T(8,128)}) fusion(f32[1024]{0:T(1024)} %param.11, bf16[1024,768]{1,0:T(8,128)(2,1)S(1)} %copy-done, bf16[768,1024]{1,0:T(8,128)(2,1)} %param.10), kind=kOutput, calls=%fused_computation.15 | convolution fusion | flops 1621098496 | bytes 9441280 | tf_op jit(solution)/shard_map/dot_general | solution.py:47
  34.7 0.0 copy-start.6
  34.7 1.3 copy-done.6
  36.1 0.0 copy-done.3
  36.1 0.0 copy-done.5
  36.1 0.7 convolution_add_fusion
  36.8 1.8 all-to-all-done
  38.6 0.2 broadcast_compare_fusion
  38.8 0.1 copy.30
  38.9 0.1 broadcast_maximum_fusion
  39.0 0.1 reshape.110
  39.1 0.1 reshape.105
  39.3 0.2 copy.34
  39.5 8.6 %gather_fusion = f32[2048,256]{1,0:T(8,128)} fusion(f32[1024,256]{1,0:T(8,128)S(1)} %convolution_add_fusion, s32[2048]{0:T(1024)S(1)} %broadcast_clamp_fusion), kind=kCustom, calls=%fused_computation | custom fusion | bytes 4202496 | tf_op jit(solution)/shard_map/jit(_take)/gather | solution.py:67
  48.1 4.2 fusion.10
  52.3 12.9 %all-to-all-start.1 = ((f32[256,1,1,8,256]{4,3,2,1,0:T(8,128)}), f32[256,1,1,8,256]{4,3,2,1,0:T(8,128)}, u32[]{:S(2)}, u32[]{:S(2)}) async-start(f32[256,1,1,8,256]{4,3,2,1,0:T(8,128)} %fusion.10), calls=%async_computation.1 | async-start | bytes 4194304 | tf_op jit(solution)/shard_map/all_to_all | solution.py:27
  65.2 0.0 all-reduce.4.cloned.1.call-start
  65.2 49.4 %all-to-all-done.1 = f32[256,1,1,8,256]{4,3,2,1,0:T(8,128)} async-done(((f32[256,1,1,8,256]{4,3,2,1,0:T(8,128)}), f32[256,1,1,8,256]{4,3,2,1,0:T(8,128)}, u32[]{:S(2)}, u32[]{:S(2)}) %all-to-all-start.1) | async-done | bytes 2097184 | tf_op jit(solution)/shard_map/all_to_all | solution.py:27
  114.6 5.1 %gather_fusion.1 = f32[1024,256]{1,0:T(8,128)S(1)} fusion(f32[2048,256]{1,0:T(8,128)} %bitcast.22, s32[1024]{0:T(1024)S(1)} %broadcast_clamp_fusion.1), kind=kCustom, calls=%fused_computation.1 | custom fusion | bytes 2101248 | tf_op jit(solution)/shard_map/jit(_take)/gather | solution.py:70
  119.7 7.5 %scatter_custom_fusion.1 = f32[2048,256]{1,0:T(8,128)} fusion(s32[1024]{0:T(1024)S(1)} %bitcast.77, f32[1024,256]{1,0:T(8,128)} %param.15, f32[]{:T(128)} %constant.32.clone.1, f32[1024,256]{1,0:T(8,128)} %param.14, f32[1024,256]{1,0:T(8,128)S(1)} %gather_fusion.1, f32[]{:T(128)} %constant.31.clone.1, pred[1024]{0:T(1024)(128)(4,1)S(1)} %get-tuple-element.39), kind=kCustom, calls=%fused_computation.25 | custom fusion | flops 786432 | bytes 5243912 | tf_op jit(solution)/shard_map/scatter | solution.py:74
  127.1 60.8 %all_to_all.15 = f32[256,1,1,8,256]{4,3,2,1,0:T(8,128)} all-to-all(f32[256,1,1,8,256]{4,3,2,1,0:T(8,128)} %bitcast.70), channel_id=1, replica_groups=mesh['code'=32,'dp'=8] {'code','dp'}, dimensions={0} | all-to-all | bytes 4194304 | tf_op jit(solution)/shard_map/all_to_all | solution.py:27
  187.9 13.1 %scatter_custom_fusion.2 = f32[1024,256]{1,0:T(8,128)} fusion(s32[2048]{0:T(1024)S(1)} %reshape.110, f32[256,1,1,8,256]{4,3,2,1,0:T(8,128)} %all_to_all.15, f32[]{:T(128)} %constant.32.clone.1), kind=kCustom, calls=%fused_computation.19 | custom fusion | flops 524288 | bytes 3145732 | tf_op jit(solution)/shard_map/scatter-add | solution.py:83
  201.0 0.0 copy-start.1
  201.0 0.0 copy-start.4
  201.0 0.0 copy-start.7
  201.0 3.8 fusion.15
  204.8 0.0 copy-done.1
  204.8 0.0 copy-done.4
  204.8 0.0 copy-done.7
  204.8 3.2 convert_reduce_fusion
  208.0 3.5 convolution_bitcast_fusion
  211.6 0.0 all-reduce.4.cloned.1.call-update
  211.6 2.8 multiply_subtract_fusion
  214.3 1.4 reduce_sum.32
  215.7 74.4 %all-reduce = (f32[1024]{0:T(1024)}, f32[256]{0:T(256)}) all-reduce(f32[1024]{0:T(1024)S(1)} %get-tuple-element.43, f32[256]{0:T(256)S(1)} %reduce_sum.32), channel_id=1, replica_groups=mesh['code'=32,'dp'=8] {'code','dp'}, use_global_device_ids=true, to_apply=%region_6.7 | all-reduce | flops 1280 | bytes 10240 | tf_op jit(solution)/shard_map/psum | solution.py:99
  290.2 190.7 %all-reduce.4.cloned.1.call-done = (f32[768,1024]{0,1:T(8,128)}, f32[1024,256]{1,0:T(8,128)}) async-done(((f32[768,1024]{0,1:T(8,128)}, f32[1024,256]{1,0:T(8,128)}), (f32[768,1024]{0,1:T(8,128)}, f32[1024,256]{1,0:T(8,128)})) %all-reduce.4.cloned.1.call-update) | async-done | bytes 4194320 | tf_op jit(solution)/shard_map/psum | solution.py:99
  480.8 0.0 copy-start.2
  480.8 3.6 copy.33
  484.5 0.0 copy-done.2
  484.5 1.0 copy.37
  (3 shorter events, 0.0 us)
Async XLA Ops:
  7.2 21.6 %copy-start = (bf16[1024,768]{1,0:T(8,128)(2,1)S(1)}, bf16[1024,768]{1,0:T(8,128)(2,1)}, u32[]{:S(2)}) copy-start(bf16[1024,768]{1,0:T(8,128)(2,1)} %param.9) | copy-start | bytes 4718596
  14.5 24.1 %all-to-all-start = ((s32[256,1,1,8]{3,2,1,0:T(1,128)}), s32[256,1,1,8]{3,2,1,0:T(1,128)S(1)}, u32[]{:S(2)}, u32[]{:S(2)}) async-start(s32[256,1,1,8]{3,2,1,0:T(1,128)} %bitcast.3), calls=%async_computation | async-start | bytes 262144 | tf_op jit(solution)/shard_map/all_to_all | solution.py:27
  28.8 7.3 %copy-start.3 = (bf16[1024,256]{1,0:T(8,128)(2,1)S(1)}, bf16[1024,256]{1,0:T(8,128)(2,1)}, u32[]{:S(2)}) copy-start(bf16[1024,256]{1,0:T(8,128)(2,1)} %param.12) | copy-start | bytes 1572868
  28.8 7.2 %copy-start.5 = (f32[256]{0:T(256)S(1)}, f32[256]{0:T(256)}, u32[]{:S(2)}) copy-start(f32[256]{0:T(256)} %param.13) | copy-start | bytes 3076
  34.7 1.3 copy-start.6
  52.3 62.3 %all-to-all-start.1 = ((f32[256,1,1,8,256]{4,3,2,1,0:T(8,128)}), f32[256,1,1,8,256]{4,3,2,1,0:T(8,128)}, u32[]{:S(2)}, u32[]{:S(2)}) async-start(f32[256,1,1,8,256]{4,3,2,1,0:T(8,128)} %fusion.10), calls=%async_computation.1 | async-start | bytes 4194304 | tf_op jit(solution)/shard_map/all_to_all | solution.py:27
  65.2 415.6 %all-reduce.4.cloned.1.call-start = ((), (), s32[]{:S(2)}) async-start(), calls=%async_computation.3 | async-start | bytes 8388608 | tf_op jit(solution)/shard_map/psum | solution.py:99
  201.0 3.8 copy-start.1
  201.0 3.8 copy-start.4
  201.0 3.8 copy-start.7
  480.8 3.6 copy-start.2
Sparse Core Ops, SparseCore 0:
  211.7 269.0 all-reduce.3
where the time goes:
time: 493 us; the launch traced here: 492 us
  waiting for transfers between devices  242 us (49%)
  blocking collectives  135 us (27%)
  other arithmetic  31.3 us (6%)
  starting transfers between devices  27.2 us (6%)
  local copies, waits for them, and re-layouts  25.3 us (5%)
  matrix products  17.1 us (3%)
  between operations  14.2 us (3%)
    psum x1, waiting for transfers between devices, per_device(): lax.psum((gw_in, gb_in, gw_out, gb_out), ('code', 'dp'))  191 us
    psum x1, blocking collectives, per_device(): lax.psum((gw_in, gb_in, gw_out, gb_out), ('code', 'dp'))  74.4 us
    all_to_all x1, blocking collectives, exchange_both(): tiles = lax.all_to_all(tiles, axis, split_axis=0, concat_axis=0, tiled=True)  60.8 us
    all_to_all x2, waiting for transfers between devices, exchange_both(): tiles = lax.all_to_all(tiles, axis, split_axis=0, concat_axis=0, tiled=True)  51.2 us
    all_to_all x2, starting transfers between devices, exchange_both(): tiles = lax.all_to_all(tiles, axis, split_axis=0, concat_axis=0, tiled=True)  27.2 us
    scatter-add x1, other arithmetic, per_device(): jax.ops.segment_sum(incoming.reshape(devices * capacity, width), row_ids,...  13.1 us
  transfers between devices with their start and end apart: 3, of which 3 were waited for; matrix products, arithmetic and copies ran while one was open for 2% of the time, Pallas kernels for 0%

commit v1 on v0

--- a/solution.py
+++ b/solution.py
@@ -96,7 +96,7 @@
         codebook, preact_grad, (((0,), (0,)), ((), ())), preferred_element_type=jnp.float32
     )
     gb_out = jnp.sum(code_grad, axis=0)
-    gw_in, gb_in, gw_out, gb_out = lax.psum((gw_in, gb_in, gw_out, gb_out), ("code", "dp"))
+    gw_in, gb_in, gw_out, gb_out = lax.psum(lax.psum((gw_in, gb_in, gw_out, gb_out), "dp"), "code")
     return (latent_grad, gw_in, gb_in, gw_out, gb_out)
 
 

time: 493 us -> 468 us (0.949)
  waiting for transfers between devices: 242 us -> 217 us
    psum x1 -> x2, waiting for transfers between devices: 191 us -> 166 us  [the longest x1 93.2 us: per_device(): lax.psum(lax.psum((gw_in, gb_in, gw_out, gb_out), 'dp'), 'code')]
    psum x1 -> x2, blocking collectives: 74.4 us -> 70.5 us  [the longest x1 56.2 us: per_device(): lax.psum(lax.psum((gw_in, gb_in, gw_out, gb_out), 'dp'), 'code')]
  transfers between devices with their start and end apart: 3 -> 4, of which waited for: 3 -> 4; matrix products, arithmetic and copies ran while one was open for 2% -> 2% of each run, Pallas kernels for 0% -> 0%
where the time goes in v1:
time: 468 us; the launch traced here: 464 us
  waiting for transfers between devices  217 us (46%)
  blocking collectives  131 us (28%)
  other arithmetic  31.3 us (7%)
  starting transfers between devices  27.3 us (6%)
  local copies, waits for them, and re-layouts  25.3 us (5%)
  matrix products  17.1 us (4%)
  between operations  14.2 us (3%)
    psum x1, waiting for transfers between devices, per_device(): lax.psum(lax.psum((gw_in, gb_in, gw_out, gb_out), 'dp'), 'code')  93.2 us
    psum x1, waiting for transfers between devices, per_device(): lax.psum((gw_in, gb_in, gw_out, gb_out), 'dp')  72.9 us
    all_to_all x1, blocking collectives, exchange_both(): tiles = lax.all_to_all(tiles, axis, split_axis=0, concat_axis=0, tiled=True)  60.8 us
    psum x1, blocking collectives, per_device(): lax.psum(lax.psum((gw_in, gb_in, gw_out, gb_out), 'dp'), 'code')  56.2 us
    all_to_all x2, waiting for transfers between devices, exchange_both(): tiles = lax.all_to_all(tiles, axis, split_axis=0, concat_axis=0, tiled=True)  51.2 us
    all_to_all x2, starting transfers between devices, exchange_both(): tiles = lax.all_to_all(tiles, axis, split_axis=0, concat_axis=0, tiled=True)  27.2 us
    psum x1, blocking collectives, per_device(): lax.psum((gw_in, gb_in, gw_out, gb_out), 'dp')  14.3 us
    scatter-add x1, other arithmetic, per_device(): jax.ops.segment_sum(incoming.reshape(devices * capacity, width), row_ids,...  13.1 us
  transfers between devices with their start and end apart: 4, of which 4 were waited for; matrix products, arithmetic and copies ran while one was open for 2% of the time, Pallas kernels for 0%

profile of v1, /device:TPU:97, one launch (start us, length us, event | category | flops | bytes accessed | tf_op | source)
XLA Modules:
  0.0 463.7 jit_solution(13004589228749882816)
XLA Ops:
  7.2 0.0 copy-start
  7.2 1.3 convert_reduce_fusion.1
  8.5 0.7 and_reduce_fusion
  9.2 4.5 scatter_custom_fusion
  13.7 0.8 reshape_transpose_transpose_reshape_reshape_reshape.6
  14.5 14.3 %all-to-all-start = ((s32[256,1,1,8]{3,2,1,0:T(1,128)}), s32[256,1,1,8]{3,2,1,0:T(1,128)S(1)}, u32[]{:S(2)}, u32[]{:S(2)}) async-start(s32[256,1,1,8]{3,2,1,0:T(1,128)} %bitcast.3), calls=%async_computation | async-start | bytes 262144 | tf_op jit(solution)/shard_map/all_to_all | solution.py:27
  28.8 0.0 copy-done
  28.8 0.0 copy-start.3
  28.8 0.0 copy-start.5
  28.8 5.9 %multiply_convert_fusion = (bf16[1024,1024]{1,0:T(8,128)(2,1)S(1)}, f32[1024,1024]{1,0:T(8,128)}) fusion(f32[1024]{0:T(1024)} %param.11, bf16[1024,768]{1,0:T(8,128)(2,1)S(1)} %copy-done, bf16[768,1024]{1,0:T(8,128)(2,1)} %param.10), kind=kOutput, calls=%fused_computation.15 | convolution fusion | flops 1621098496 | bytes 9441280 | tf_op jit(solution)/shard_map/dot_general | solution.py:47
  34.7 0.0 copy-start.6
  34.7 1.3 copy-done.6
  36.1 0.0 copy-done.3
  36.1 0.0 copy-done.5
  36.1 0.7 convolution_add_fusion
  36.8 1.8 all-to-all-done
  38.6 0.2 broadcast_compare_fusion
  38.8 0.1 copy.30
  38.9 0.1 broadcast_maximum_fusion
  39.0 0.1 reshape.110
  39.1 0.1 reshape.105
  39.3 0.2 copy.34
  39.5 8.6 %gather_fusion = f32[2048,256]{1,0:T(8,128)} fusion(f32[1024,256]{1,0:T(8,128)S(1)} %convolution_add_fusion, s32[2048]{0:T(1024)S(1)} %broadcast_clamp_fusion), kind=kCustom, calls=%fused_computation | custom fusion | bytes 4202496 | tf_op jit(solution)/shard_map/jit(_take)/gather | solution.py:67
  48.1 4.2 fusion.10
  52.3 12.9 %all-to-all-start.1 = ((f32[256,1,1,8,256]{4,3,2,1,0:T(8,128)}), f32[256,1,1,8,256]{4,3,2,1,0:T(8,128)}, u32[]{:S(2)}, u32[]{:S(2)}) async-start(f32[256,1,1,8,256]{4,3,2,1,0:T(8,128)} %fusion.10), calls=%async_computation.1 | async-start | bytes 4194304 | tf_op jit(solution)/shard_map/all_to_all | solution.py:27
  65.2 0.0 all-reduce.9.cloned.1.call-start
  65.2 49.4 %all-to-all-done.1 = f32[256,1,1,8,256]{4,3,2,1,0:T(8,128)} async-done(((f32[256,1,1,8,256]{4,3,2,1,0:T(8,128)}), f32[256,1,1,8,256]{4,3,2,1,0:T(8,128)}, u32[]{:S(2)}, u32[]{:S(2)}) %all-to-all-start.1) | async-done | bytes 2097184 | tf_op jit(solution)/shard_map/all_to_all | solution.py:27
  114.6 5.1 %gather_fusion.1 = f32[1024,256]{1,0:T(8,128)S(1)} fusion(f32[2048,256]{1,0:T(8,128)} %bitcast.22, s32[1024]{0:T(1024)S(1)} %broadcast_clamp_fusion.1), kind=kCustom, calls=%fused_computation.1 | custom fusion | bytes 2101248 | tf_op jit(solution)/shard_map/jit(_take)/gather | solution.py:70
  119.7 7.5 %scatter_custom_fusion.1 = f32[2048,256]{1,0:T(8,128)} fusion(s32[1024]{0:T(1024)S(1)} %bitcast.77, f32[1024,256]{1,0:T(8,128)} %param.15, f32[]{:T(128)} %constant.32.clone.1, f32[1024,256]{1,0:T(8,128)} %param.14, f32[1024,256]{1,0:T(8,128)S(1)} %gather_fusion.1, f32[]{:T(128)} %constant.31.clone.1, pred[1024]{0:T(1024)(128)(4,1)S(1)} %get-tuple-element.43), kind=kCustom, calls=%fused_computation.25 | custom fusion | flops 786432 | bytes 5243912 | tf_op jit(solution)/shard_map/scatter | solution.py:74
  127.1 60.8 %all_to_all.15 = f32[256,1,1,8,256]{4,3,2,1,0:T(8,128)} all-to-all(f32[256,1,1,8,256]{4,3,2,1,0:T(8,128)} %bitcast.70), channel_id=1, replica_groups=mesh['code'=32,'dp'=8] {'code','dp'}, dimensions={0} | all-to-all | bytes 4194304 | tf_op jit(solution)/shard_map/all_to_all | solution.py:27
  187.9 13.1 %scatter_custom_fusion.2 = f32[1024,256]{1,0:T(8,128)} fusion(s32[2048]{0:T(1024)S(1)} %reshape.110, f32[256,1,1,8,256]{4,3,2,1,0:T(8,128)} %all_to_all.15, f32[]{:T(128)} %constant.32.clone.1), kind=kCustom, calls=%fused_computation.19 | custom fusion | flops 524288 | bytes 3145732 | tf_op jit(solution)/shard_map/scatter-add | solution.py:83
  201.0 0.0 copy-start.1
  201.0 0.0 copy-start.4
  201.0 0.0 copy-start.7
  201.0 3.7 fusion.15
  204.7 0.0 copy-done.1
  204.7 0.0 copy-done.4
  204.7 0.0 copy-done.7
  204.7 3.2 convert_reduce_fusion
  208.0 3.6 convolution_bitcast_fusion
  211.5 0.0 all-reduce.9.cloned.1.call-update
  211.6 0.0 all-reduce.7.cloned.1.call-start
  211.6 72.9 %all-reduce.9.cloned.1.call-done = (f32[768,1024]{0,1:T(8,128)}, f32[1024,256]{1,0:T(8,128)}) async-done(((f32[768,1024]{0,1:T(8,128)}, f32[1024,256]{1,0:T(8,128)}), (f32[768,1024]{0,1:T(8,128)}, f32[1024,256]{1,0:T(8,128)})) %all-reduce.9.cloned.1.call-update) | async-done | bytes 4194320 | tf_op jit(solution)/shard_map/psum | solution.py:99
  284.5 0.0 all-reduce.7.cloned.1.call-update
  284.5 2.8 multiply_subtract_fusion
  287.3 1.4 reduce_sum.32
  288.6 14.3 %all-reduce.2 = (f32[1024]{0:T(1024)S(1)}, f32[256]{0:T(256)S(1)}) all-reduce(f32[1024]{0:T(1024)S(1)} %get-tuple-element.47, f32[256]{0:T(256)S(1)} %reduce_sum.32), channel_id=1, replica_groups=mesh['code'=32,'dp'=8] {'dp'}, use_global_device_ids=true, to_apply=%region_7.8 | all-reduce | flops 1280 | bytes 10240 | tf_op jit(solution)/shard_map/psum | solution.py:99
  302.9 56.2 %all-reduce = (f32[1024]{0:T(1024)}, f32[256]{0:T(256)}) all-reduce(f32[1024]{0:T(1024)S(1)} %get-tuple-element.39, f32[256]{0:T(256)S(1)} %get-tuple-element.40), channel_id=1, replica_groups=mesh['code'=32,'dp'=8] {'code'}, use_global_device_ids=true, to_apply=%region_8.9 | all-reduce | flops 1280 | bytes 10240 | tf_op jit(solution)/shard_map/psum | solution.py:99
  359.1 93.2 %all-reduce.7.cloned.1.call-done = (f32[768,1024]{0,1:T(8,128)}, f32[1024,256]{1,0:T(8,128)}) async-done(((f32[768,1024]{0,1:T(8,128)}, f32[1024,256]{1,0:T(8,128)}), (f32[768,1024]{0,1:T(8,128)}, f32[1024,256]{1,0:T(8,128)})) %all-reduce.7.cloned.1.call-update) | async-done | bytes 4194320 | tf_op jit(solution)/shard_map/psum | solution.py:99
  452.3 0.0 copy-start.2
  452.3 3.6 copy.33
  455.9 0.0 copy-done.2
  455.9 1.0 copy.39
  (3 shorter events, 0.0 us)
Async XLA Ops:
  7.2 21.6 %copy-start = (bf16[1024,768]{1,0:T(8,128)(2,1)S(1)}, bf16[1024,768]{1,0:T(8,128)(2,1)}, u32[]{:S(2)}) copy-start(bf16[1024,768]{1,0:T(8,128)(2,1)} %param.9) | copy-start | bytes 4718596
  14.5 24.1 %all-to-all-start = ((s32[256,1,1,8]{3,2,1,0:T(1,128)}), s32[256,1,1,8]{3,2,1,0:T(1,128)S(1)}, u32[]{:S(2)}, u32[]{:S(2)}) async-start(s32[256,1,1,8]{3,2,1,0:T(1,128)} %bitcast.3), calls=%async_computation | async-start | bytes 262144 | tf_op jit(solution)/shard_map/all_to_all | solution.py:27
  28.8 7.3 %copy-start.3 = (bf16[1024,256]{1,0:T(8,128)(2,1)S(1)}, bf16[1024,256]{1,0:T(8,128)(2,1)}, u32[]{:S(2)}) copy-start(bf16[1024,256]{1,0:T(8,128)(2,1)} %param.12) | copy-start | bytes 1572868
  28.8 7.2 %copy-start.5 = (f32[256]{0:T(256)S(1)}, f32[256]{0:T(256)}, u32[]{:S(2)}) copy-start(f32[256]{0:T(256)} %param.13) | copy-start | bytes 3076
  34.7 1.3 copy-start.6
  52.3 62.3 %all-to-all-start.1 = ((f32[256,1,1,8,256]{4,3,2,1,0:T(8,128)}), f32[256,1,1,8,256]{4,3,2,1,0:T(8,128)}, u32[]{:S(2)}, u32[]{:S(2)}) async-start(f32[256,1,1,8,256]{4,3,2,1,0:T(8,128)} %fusion.10), calls=%async_computation.1 | async-start | bytes 4194304 | tf_op jit(solution)/shard_map/all_to_all | solution.py:27
  65.2 219.3 %all-reduce.9.cloned.1.call-start = ((), (), s32[]{:S(2)}) async-start(), calls=%async_computation.4 | async-start | bytes 8388608 | tf_op jit(solution)/shard_map/psum | solution.py:99
  201.0 3.7 copy-start.1
  201.0 3.7 copy-start.4
  201.0 3.7 copy-start.7
  211.6 240.7 %all-reduce.7.cloned.1.call-start = ((), (), s32[]{:S(2)}) async-start(), calls=%async_computation.3 | async-start | bytes 8388608 | tf_op jit(solution)/shard_map/psum | solution.py:99
  452.3 3.6 copy-start.2
Sparse Core Ops, SparseCore 0:
  211.7 72.7 all-reduce.8
  288.2 164.0 all-reduce.6
